TPU v7x, 32 devices: a whole 2x2x4 slice. The times are simulated.
32 devices in a mesh: groups: 2 (over y), grow: 4 (over z), cross: 2 (over x), side: 2 (over core).
Axes of the slice: x: 2, y: 2, z: 4, core: 2. Of those that a mesh axis runs over, the one named last changes fastest.
Arguments:
- phase_field: float32 [32, 64, 1024], P(('groups', 'grow'), 'cross', 'side'), parts along dimension 0, may hold values from -1.1 to 1.1
- solute_field: float32 [32, 64, 1024], P(('groups', 'grow'), 'cross', 'side'), parts along dimension 0, may hold values from -1 to 0.2
- shift_step: int32 [2], P('groups'), parts along dimension 0, may hold values from 0 to 1
- inflow_seed: int32 [128, 1024], P(('groups', 'cross'), 'side'), parts along dimension 0, may hold values from 0 to 1023
Outputs:
- phase_out: float32 [32, 64, 1024], P(('groups', 'grow'), 'cross', 'side'), parts along dimension 0
- solute_out: float32 [32, 64, 1024], P(('groups', 'grow'), 'cross', 'side'), parts along dimension 0
There are 2 independent parts, one for each index of `groups`. A program takes and returns all parts, laid end to end along the dimension named above; each array names one. Nothing has to cross between parts.
Inputs may be any that keep to these rules, and one draw needn't show every extreme that they name: `shift_step`: the frame moves once, between two of the 3 steps.
All inputs are finite; a program needn't handle non-finite values.
Results may differ from a plain program's by a relative error of at most 0.00002.
Values sent between devices are 32-bit elements; how exact they have to be, the bound alone decides.
A program may use at most 64 MiB of HBM per device.

v0:
```python
import jax
import jax.numpy as jnp
from jax import lax
from jax.sharding import PartitionSpec as P

ITERS = 3


partition = 0.15
coupling = 2.0
diffusion = 2.0
spacing_sq = 0.64
time_step = 0.025
gradient_scale = 1.2
drift_rate = 0.01
seed_levels = 1024.0


def extended(shard, sides, width, wrap):
    for axis, dim in sides:
        size, length = (lax.axis_size(axis), shard.shape[dim])
        up = [(i, (i + 1) % size) for i in range(size if wrap else size - 1)]
        down = [(j, i) for i, j in up]
        last = lax.slice_in_dim(shard, length - width, length, axis=dim)
        first = lax.slice_in_dim(shard, 0, width, axis=dim)
        before = lax.ppermute(last, axis, up)
        after = lax.ppermute(first, axis, down)
        shard = jnp.concatenate([before, shard, after], axis=dim)
    return shard


def passed_along(shard, axis, by):
    size = lax.axis_size(axis)
    pairs = [(i, i + by) for i in range(size) if 0 <= i + by < size]
    return lax.ppermute(shard, axis, pairs)


def neighbours(side_pad, growth_pad):
    return [
        growth_pad[:, :-2],
        growth_pad[:, 2:],
        side_pad[:, :, :-2, 1:-1],
        side_pad[:, :, 2:, 1:-1],
        side_pad[:, :, 1:-1, :-2],
        side_pad[:, :, 1:-1, 2:],
    ]


def advance(center, nearby, temper):
    phases = center[0]
    solutes = center[1]
    laplace = -6.0 * phases
    for entry in nearby:
        laplace = laplace + entry[0]
    laplace = laplace / spacing_sq
    slowing = 1.0 - (1.0 - partition) * temper
    driving = (
        laplace
        + phases
        - phases * phases * phases
        - coupling * (1.0 - phases * phases) ** 2 * (solutes + temper)
    )
    growth_rate = driving / slowing
    clipped = jnp.clip(phases, -1.0, 1.0)
    mobile = 0.5 * (1.0 - clipped)
    current = jnp.zeros_like(phases)
    for entry in nearby:
        near_mobile = 0.5 * (1.0 - jnp.clip(entry[0], -1.0, 1.0))
        current = current + 0.5 * (mobile + near_mobile) * (entry[1] - solutes)
    current = current * (diffusion / spacing_sq)
    weight = 0.5 * (1.0 + partition - (1.0 - partition) * clipped)
    solute_rate = (current + 0.5 * (1.0 + (1.0 - partition) * solutes) * growth_rate) / weight
    return jnp.stack([phases + time_step * growth_rate, solutes + time_step * solute_rate])


def mirror_ends(padded, at_bottom, at_top):
    lower_row = jnp.where(at_bottom, padded[:, 1:2], padded[:, 0:1])
    upper_row = jnp.where(at_top, padded[:, -2:-1], padded[:, -1:])
    return jnp.concatenate([lower_row, padded[:, 1:-1], upper_row], 1)


def cross_pad(fields):
    return extended(fields, (("cross", 2), ("side", 3)), 1, True)


def shards(phase_field, solute_field, shift_step, inflow_seed):
    grow_index = lax.axis_index("grow")
    grow_last = lax.axis_size("grow") - 1
    at_bottom = grow_index == 0
    at_top = grow_index == grow_last
    planes = phase_field.shape[0]
    grid_rows = planes * lax.axis_size("grow")
    frame_step = shift_step[0]
    inflow = inflow_seed.astype(jnp.float32) / seed_levels - 1.0
    top_pair = jnp.stack([jnp.full_like(inflow, -1.0), inflow])[:, None]
    fields = jnp.stack([phase_field, solute_field])
    heights = (grow_index * planes + jnp.arange(planes)).astype(jnp.float32)[:, None, None]
    for step_index in range(ITERS):
        window = extended(fields, (("grow", 1),), 1, False)
        window = mirror_ends(window, at_bottom, at_top)
        side_pad = cross_pad(fields)
        nearby = neighbours(side_pad, window)
        shifts = (frame_step < step_index).astype(jnp.float32)
        temper = (
            gradient_scale * ((heights + shifts + 0.5) / grid_rows - 0.5) - drift_rate * step_index
        )
        fields = advance(side_pad[:, :, 1:-1, 1:-1], nearby, temper)
        if step_index < ITERS - 1:
            handed = passed_along(fields[:, :1], "grow", -1)
            handed = jnp.where(at_top, top_pair, handed)
            shifted = jnp.concatenate([fields[:, 1:], handed], 1)
            fields = jnp.where(frame_step == step_index, shifted, fields)
    return (fields[0], fields[1])


def solution(mesh):
    return jax.shard_map(
        shards,
        mesh=mesh,
        in_specs=(
            P(("groups", "grow"), "cross", "side"),
            P(("groups", "grow"), "cross", "side"),
            P("groups"),
            P(("groups", "cross"), "side"),
        ),
        out_specs=(P(("groups", "grow"), "cross", "side"), P(("groups", "grow"), "cross", "side")),
        check_vma=False,
    )
```

profile of v0, /device:TPU:0, one launch (start us, length us, event | category | flops | bytes accessed | tf_op | source)
XLA Modules:
  0.0 62.9 jit_solution(1464265654475939014)
XLA Ops:
  0.6 0.9 %fusion.95 = f32[2,1,32,512]{3,2,1,0:T(8,128)S(1)} fusion(f32[1,4,32,512]{3,2,1,0:T(8,128)} %bitcast.254, f32[1,4,32,512]{3,2,1,0:T(8,128)} %bitcast.248), kind=kLoop, calls=%fused_computation.192 | loop fusion | flops 32768 | bytes 655360 | tf_op jit(solution)/shard_map/stack | solution.py:96
  1.6 5.0 %collective-permute-start = (f32[2,1,32,512]{3,2,1,0:T(8,128)S(1)}, f32[2,1,32,512]{3,2,1,0:T(8,128)S(1)}, u32[]{:S(2)}, u32[]{:S(2)}) collective-permute-start(f32[2,1,32,512]{3,2,1,0:T(8,128)S(1)} %fusion.95), channel_id=1, source_target_pairs={{0,4},{4,8},{8,12},{1,5},{5,9},{9,13},{2,6},{6,10},{10,14},{3,7},{... | collective-permute-start | bytes 393224 | tf_op jit(solution)/shard_map/ppermute | solution.py:26
  6.6 1.6 %collective-permute-start.2 = (f32[2,4,1,512]{3,2,1,0:T(1,128)S(1)}, f32[2,4,1,512]{3,2,1,0:T(1,128)S(1)}, u32[]{:S(2)}, u32[]{:S(2)}) collective-permute-start(f32[2,4,1,512]{3,2,1,0:T(1,128)S(1)} %get-tuple-element.26), channel_id=1, source_target_pairs={{0,2},{2,0},{1,3},{3,1},{4,6},{6,4},{5,7},{7,5},{8,10},{10,8},{9,1... | collective-permute-start | bytes 49160 | tf_op jit(solution)/shard_map/ppermute | solution.py:26
  9.4 1.3 %collective-permute-start.1 = (f32[2,1,32,512]{3,2,1,0:T(8,128)S(1)}, f32[2,1,32,512]{3,2,1,0:T(8,128)S(1)}, u32[]{:S(2)}, u32[]{:S(2)}) collective-permute-start(f32[2,1,32,512]{3,2,1,0:T(8,128)S(1)} %get-tuple-element.7), channel_id=1, source_target_pairs={{4,0},{8,4},{12,8},{5,1},{9,5},{13,9},{6,2},{10,6},{14,10},{7,3},{... | collective-permute-start | bytes 393224 | tf_op jit(solution)/shard_map/ppermute | solution.py:27
  10.7 1.2 %collective-permute-done.3 = f32[2,4,1,512]{3,2,1,0:T(1,128)S(1)} collective-permute-done((f32[2,4,1,512]{3,2,1,0:T(1,128)S(1)}, f32[2,4,1,512]{3,2,1,0:T(1,128)S(1)}, u32[]{:S(2)}, u32[]{:S(2)}) %collective-permute-start.3) | collective-permute-done | bytes 16416 | tf_op jit(solution)/shard_map/ppermute | solution.py:27
  12.6 4.0 %collective-permute-done.1 = f32[2,1,32,512]{3,2,1,0:T(8,128)S(1)} collective-permute-done((f32[2,1,32,512]{3,2,1,0:T(8,128)S(1)}, f32[2,1,32,512]{3,2,1,0:T(8,128)S(1)}, u32[]{:S(2)}, u32[]{:S(2)}) %collective-permute-start.1) | collective-permute-done | bytes 131104 | tf_op jit(solution)/shard_map/ppermute | solution.py:27
  17.0 1.0 %add_bitcast_fusion = f32[1,4,32,512]{3,2,1,0:T(8,128)S(1)} fusion(f32[4,32,512]{2,1,0:T(8,128)S(1)} %copy-done, f32[2,4,34,1]{3,2,1,0:T(8,128)S(1)} %collective-permute-done.5, f32[2,4,1,512]{3,2,1,0:T(1,128)S(1)} %collective-permute-done.3, f32[1,4,32,512]{3,2,1,0:T(8,128)S(1)} %bitcast.253, f32[1,4,32,512]{3,2,1,0:T(8,128)S(1)} %bitcast.259, ...), kind=kLoop, calls=%fused_computation.178 | loop fusion | flops 7405568 | bytes 1607840 | tf_op jit(solution)/shard_map/stack | solution.py:73
  18.0 1.3 %collective-permute-start.6 = (f32[2,1,32,512]{3,2,1,0:T(8,128)S(1)}, f32[2,1,32,512]{3,2,1,0:T(8,128)S(1)}, u32[]{:S(2)}, u32[]{:S(2)}) collective-permute-start(f32[2,1,32,512]{3,2,1,0:T(8,128)S(1)} %fusion.97), channel_id=1, source_target_pairs={{4,0},{8,4},{12,8},{5,1},{9,5},{13,9},{6,2},{10,6},{14,10},{7,3},{... | collective-permute-start | bytes 393224 | tf_op jit(solution)/shard_map/ppermute | solution.py:35
  19.4 5.5 %collective-permute-done.6 = f32[2,1,32,512]{3,2,1,0:T(8,128)S(1)} collective-permute-done((f32[2,1,32,512]{3,2,1,0:T(8,128)S(1)}, f32[2,1,32,512]{3,2,1,0:T(8,128)S(1)}, u32[]{:S(2)}, u32[]{:S(2)}) %collective-permute-start.6) | collective-permute-done | bytes 131104 | tf_op jit(solution)/shard_map/ppermute | solution.py:35
  25.1 3.9 %collective-permute-start.7 = (f32[2,1,32,512]{3,2,1,0:T(8,128)S(1)}, f32[2,1,32,512]{3,2,1,0:T(8,128)S(1)}, u32[]{:S(2)}, u32[]{:S(2)}) collective-permute-start(f32[2,1,32,512]{3,2,1,0:T(8,128)S(1)} %get-tuple-element.22), channel_id=1, source_target_pairs={{0,4},{4,8},{8,12},{1,5},{5,9},{9,13},{2,6},{6,10},{10,14},{3,7},{... | collective-permute-start | bytes 393224 | tf_op jit(solution)/shard_map/ppermute | solution.py:26
  29.0 1.3 %collective-permute-start.8 = (f32[2,1,32,512]{3,2,1,0:T(8,128)S(1)}, f32[2,1,32,512]{3,2,1,0:T(8,128)S(1)}, u32[]{:S(2)}, u32[]{:S(2)}) collective-permute-start(f32[2,1,32,512]{3,2,1,0:T(8,128)S(1)} %get-tuple-element.23), channel_id=1, source_target_pairs={{4,0},{8,4},{12,8},{5,1},{9,5},{13,9},{6,2},{10,6},{14,10},{7,3},{... | collective-permute-start | bytes 393224 | tf_op jit(solution)/shard_map/ppermute | solution.py:27
  30.3 1.6 %collective-permute-start.10 = (f32[2,4,1,512]{3,2,1,0:T(1,128)S(1)}, f32[2,4,1,512]{3,2,1,0:T(1,128)S(1)}, u32[]{:S(2)}, u32[]{:S(2)}) collective-permute-start(f32[2,4,1,512]{3,2,1,0:T(1,128)S(1)} %get-tuple-element.25), channel_id=1, source_target_pairs={{2,0},{0,2},{3,1},{1,3},{6,4},{4,6},{7,5},{5,7},{10,8},{8,10},{11,... | collective-permute-start | bytes 49160 | tf_op jit(solution)/shard_map/ppermute | solution.py:27
  32.4 1.7 %collective-permute-done.10 = f32[2,4,1,512]{3,2,1,0:T(1,128)S(1)} collective-permute-done((f32[2,4,1,512]{3,2,1,0:T(1,128)S(1)}, f32[2,4,1,512]{3,2,1,0:T(1,128)S(1)}, u32[]{:S(2)}, u32[]{:S(2)}) %collective-permute-start.10) | collective-permute-done | bytes 16416 | tf_op jit(solution)/shard_map/ppermute | solution.py:27
  34.1 1.5 %collective-permute-done.9 = f32[2,4,1,512]{3,2,1,0:T(1,128)S(1)} collective-permute-done((f32[2,4,1,512]{3,2,1,0:T(1,128)S(1)}, f32[2,4,1,512]{3,2,1,0:T(1,128)S(1)}, u32[]{:S(2)}, u32[]{:S(2)}) %collective-permute-start.9) | collective-permute-done | bytes 16416 | tf_op jit(solution)/shard_map/ppermute | solution.py:26
  36.4 0.8 %collective-permute-done.11 = f32[2,4,34,1]{3,2,1,0:T(8,128)S(1)} collective-permute-done((f32[2,4,34,1]{3,2,1,0:T(8,128)S(1)}, f32[2,4,34,1]{3,2,1,0:T(8,128)S(1)}, u32[]{:S(2)}, u32[]{:S(2)}) %collective-permute-start.11) | collective-permute-done | bytes 1120 | tf_op jit(solution)/shard_map/ppermute | solution.py:26
  37.8 1.0 %multiply_add_fusion.2 = f32[1,4,32,512]{3,2,1,0:T(8,128)S(1)} fusion(f32[2,4,34,1]{3,2,1,0:T(8,128)S(1)} %collective-permute-done.12, f32[2,4,1,512]{3,2,1,0:T(1,128)S(1)} %collective-permute-done.10, f32[2,4,32,512]{3,2,1,0:T(8,128)S(1)} %fusion.1, f32[2,4,1,512]{3,2,1,0:T(1,128)S(1)} %collective-permute-done.9, ...), kind=kLoop, calls=%fused_computation.175 | loop fusion | flops 6619136 | bytes 1934336 | tf_op jit(solution)/shard_map/add | solution.py:73
  38.8 1.3 %collective-permute-start.13 = (f32[2,1,32,512]{3,2,1,0:T(8,128)S(1)}, f32[2,1,32,512]{3,2,1,0:T(8,128)S(1)}, u32[]{:S(2)}, u32[]{:S(2)}) collective-permute-start(f32[2,1,32,512]{3,2,1,0:T(8,128)S(1)} %fusion.96), channel_id=1, source_target_pairs={{4,0},{8,4},{12,8},{5,1},{9,5},{13,9},{6,2},{10,6},{14,10},{7,3},{... | collective-permute-start | bytes 393224 | tf_op jit(solution)/shard_map/ppermute | solution.py:35
  40.2 7.1 %collective-permute-done.13 = f32[2,1,32,512]{3,2,1,0:T(8,128)S(1)} collective-permute-done((f32[2,1,32,512]{3,2,1,0:T(8,128)S(1)}, f32[2,1,32,512]{3,2,1,0:T(8,128)S(1)}, u32[]{:S(2)}, u32[]{:S(2)}) %collective-permute-start.13) | collective-permute-done | bytes 131104 | tf_op jit(solution)/shard_map/ppermute | solution.py:35
  48.1 1.5 %collective-permute-start.17 = (f32[2,4,1,512]{3,2,1,0:T(1,128)S(1)}, f32[2,4,1,512]{3,2,1,0:T(1,128)S(1)}, u32[]{:S(2)}, u32[]{:S(2)}) collective-permute-start(f32[2,4,1,512]{3,2,1,0:T(1,128)S(1)} %get-tuple-element.18), channel_id=1, source_target_pairs={{2,0},{0,2},{3,1},{1,3},{6,4},{4,6},{7,5},{5,7},{10,8},{8,10},{11,... | collective-permute-start | bytes 49160 | tf_op jit(solution)/shard_map/ppermute | solution.py:27
  49.6 3.6 %collective-permute-start.14 = (f32[2,1,32,512]{3,2,1,0:T(8,128)S(1)}, f32[2,1,32,512]{3,2,1,0:T(8,128)S(1)}, u32[]{:S(2)}, u32[]{:S(2)}) collective-permute-start(f32[2,1,32,512]{3,2,1,0:T(8,128)S(1)} %get-tuple-element.17), channel_id=1, source_target_pairs={{0,4},{4,8},{8,12},{1,5},{5,9},{9,13},{2,6},{6,10},{10,14},{3,7},{... | collective-permute-start | bytes 393224 | tf_op jit(solution)/shard_map/ppermute | solution.py:26
  53.2 1.3 %collective-permute-start.15 = (f32[2,1,32,512]{3,2,1,0:T(8,128)S(1)}, f32[2,1,32,512]{3,2,1,0:T(8,128)S(1)}, u32[]{:S(2)}, u32[]{:S(2)}) collective-permute-start(f32[2,1,32,512]{3,2,1,0:T(8,128)S(1)} %get-tuple-element.16), channel_id=1, source_target_pairs={{4,0},{8,4},{12,8},{5,1},{9,5},{13,9},{6,2},{10,6},{14,10},{7,3},{... | collective-permute-start | bytes 393224 | tf_op jit(solution)/shard_map/ppermute | solution.py:27
  55.7 4.4 %collective-permute-done.15 = f32[2,1,32,512]{3,2,1,0:T(8,128)S(1)} collective-permute-done((f32[2,1,32,512]{3,2,1,0:T(8,128)S(1)}, f32[2,1,32,512]{3,2,1,0:T(8,128)S(1)}, u32[]{:S(2)}, u32[]{:S(2)}) %collective-permute-start.15) | collective-permute-done | bytes 131104 | tf_op jit(solution)/shard_map/ppermute | solution.py:27
  60.1 1.7 %multiply_add_fusion = f32[4,32,512]{2,1,0:T(8,128)} fusion(f32[2,4,34,1]{3,2,1,0:T(8,128)S(1)} %collective-permute-done.19, f32[2,4,1,512]{3,2,1,0:T(1,128)S(1)} %collective-permute-done.17, f32[2,4,32,512]{3,2,1,0:T(8,128)S(1)} %fusion, f32[2,4,1,512]{3,2,1,0:T(1,128)S(1)} %collective-permute-done.16, f32[2,4,34,1]{3,2,1,0:T(8,128)S(1)} %collective-permute-done.18, ...), kind=kLoop, calls=%fused_computation.172 | loop fusion | flops 6619136 | bytes 1934336 | tf_op jit(solution)/shard_map/add | solution.py:73
  61.8 1.0 %multiply_add_fusion.1 = f32[4,32,512]{2,1,0:T(8,128)} fusion(f32[2,4,32,512]{3,2,1,0:T(8,128)S(1)} %fusion, f32[4]{0:T(128)S(1)} %get-tuple-element.2, f32[4]{0:T(128)S(1)} %get-tuple-element.3, f32[2,4,1,512]{3,2,1,0:T(1,128)S(1)} %collective-permute-done.16, f32[2,4,1,512]{3,2,1,0:T(1,128)S(1)} %collective-permute-done.17, ...), kind=kLoop, calls=%fused_computation.173 | loop fusion | flops 2031616 | bytes 1934336 | tf_op jit(solution)/shard_map/add | solution.py:73
  (53 shorter events, 5.7 us)
Async XLA Ops:
  0.6 5.9 %copy-start = (f32[4,32,512]{2,1,0:T(8,128)S(1)}, f32[4,32,512]{2,1,0:T(8,128)}, u32[]{:S(2)}) copy-start(f32[4,32,512]{2,1,0:T(8,128)} %param.5) | copy-start | bytes 786436
  0.6 5.9 %copy-start.1 = (f32[4,32,512]{2,1,0:T(8,128)S(1)}, f32[4,32,512]{2,1,0:T(8,128)}, u32[]{:S(2)}) copy-start(f32[4,32,512]{2,1,0:T(8,128)} %param.4) | copy-start | bytes 786436
  1.6 7.8 %collective-permute-start = (f32[2,1,32,512]{3,2,1,0:T(8,128)S(1)}, f32[2,1,32,512]{3,2,1,0:T(8,128)S(1)}, u32[]{:S(2)}, u32[]{:S(2)}) collective-permute-start(f32[2,1,32,512]{3,2,1,0:T(8,128)S(1)} %fusion.95), channel_id=1, source_target_pairs={{0,4},{4,8},{8,12},{1,5},{5,9},{9,13},{2,6},{6,10},{10,14},{3,7},{... | collective-permute-start | bytes 393224 | tf_op jit(solution)/shard_map/ppermute | solution.py:26
  6.6 4.1 %collective-permute-start.2 = (f32[2,4,1,512]{3,2,1,0:T(1,128)S(1)}, f32[2,4,1,512]{3,2,1,0:T(1,128)S(1)}, u32[]{:S(2)}, u32[]{:S(2)}) collective-permute-start(f32[2,4,1,512]{3,2,1,0:T(1,128)S(1)} %get-tuple-element.26), channel_id=1, source_target_pairs={{0,2},{2,0},{1,3},{3,1},{4,6},{6,4},{5,7},{7,5},{8,10},{10,8},{9,1... | collective-permute-start | bytes 49160 | tf_op jit(solution)/shard_map/ppermute | solution.py:26
  8.2 3.7 %collective-permute-start.3 = (f32[2,4,1,512]{3,2,1,0:T(1,128)S(1)}, f32[2,4,1,512]{3,2,1,0:T(1,128)S(1)}, u32[]{:S(2)}, u32[]{:S(2)}) collective-permute-start(f32[2,4,1,512]{3,2,1,0:T(1,128)S(1)} %get-tuple-element.27), channel_id=1, source_target_pairs={{2,0},{0,2},{3,1},{1,3},{6,4},{4,6},{7,5},{5,7},{10,8},{8,10},{11,... | collective-permute-start | bytes 49160 | tf_op jit(solution)/shard_map/ppermute | solution.py:27
  9.4 7.2 %collective-permute-start.1 = (f32[2,1,32,512]{3,2,1,0:T(8,128)S(1)}, f32[2,1,32,512]{3,2,1,0:T(8,128)S(1)}, u32[]{:S(2)}, u32[]{:S(2)}) collective-permute-start(f32[2,1,32,512]{3,2,1,0:T(8,128)S(1)} %get-tuple-element.7), channel_id=1, source_target_pairs={{4,0},{8,4},{12,8},{5,1},{9,5},{13,9},{6,2},{10,6},{14,10},{7,3},{... | collective-permute-start | bytes 393224 | tf_op jit(solution)/shard_map/ppermute | solution.py:27
  12.0 4.6 %collective-permute-start.4 = (f32[2,4,34,1]{3,2,1,0:T(8,128)S(1)}, f32[2,4,34,1]{3,2,1,0:T(8,128)S(1)}, u32[]{:S(2)}, u32[]{:S(2)}) collective-permute-start(f32[2,4,34,1]{3,2,1,0:T(8,128)S(1)} %get-tuple-element.12), channel_id=1, source_target_pairs={{0,1},{1,0},{2,3},{3,2},{4,5},{5,4},{6,7},{7,6},{8,9},{9,8},{10,11... | collective-permute-start | bytes 3272 | tf_op jit(solution)/shard_map/ppermute | solution.py:26
  12.1 4.6 %collective-permute-start.5 = (f32[2,4,34,1]{3,2,1,0:T(8,128)S(1)}, f32[2,4,34,1]{3,2,1,0:T(8,128)S(1)}, u32[]{:S(2)}, u32[]{:S(2)}) collective-permute-start(f32[2,4,34,1]{3,2,1,0:T(8,128)S(1)} %get-tuple-element.13), channel_id=1, source_target_pairs={{1,0},{0,1},{3,2},{2,3},{5,4},{4,5},{7,6},{6,7},{9,8},{8,9},{11,10... | collective-permute-start | bytes 3272 | tf_op jit(solution)/shard_map/ppermute | solution.py:27
  18.0 1.3 %copy-start.2 = (s32[32,512]{1,0:T(8,128)S(1)}, s32[32,512]{1,0:T(8,128)}, u32[]{:S(2)}) copy-start(s32[32,512]{1,0:T(8,128)} %param.7) | copy-start | bytes 196612
  18.0 6.9 %collective-permute-start.6 = (f32[2,1,32,512]{3,2,1,0:T(8,128)S(1)}, f32[2,1,32,512]{3,2,1,0:T(8,128)S(1)}, u32[]{:S(2)}, u32[]{:S(2)}) collective-permute-start(f32[2,1,32,512]{3,2,1,0:T(8,128)S(1)} %fusion.97), channel_id=1, source_target_pairs={{4,0},{8,4},{12,8},{5,1},{9,5},{13,9},{6,2},{10,6},{14,10},{7,3},{... | collective-permute-start | bytes 393224 | tf_op jit(solution)/shard_map/ppermute | solution.py:35
  25.1 11.2 %collective-permute-start.7 = (f32[2,1,32,512]{3,2,1,0:T(8,128)S(1)}, f32[2,1,32,512]{3,2,1,0:T(8,128)S(1)}, u32[]{:S(2)}, u32[]{:S(2)}) collective-permute-start(f32[2,1,32,512]{3,2,1,0:T(8,128)S(1)} %get-tuple-element.22), channel_id=1, source_target_pairs={{0,4},{4,8},{8,12},{1,5},{5,9},{9,13},{2,6},{6,10},{10,14},{3,7},{... | collective-permute-start | bytes 393224 | tf_op jit(solution)/shard_map/ppermute | solution.py:26
  29.0 7.3 %collective-permute-start.8 = (f32[2,1,32,512]{3,2,1,0:T(8,128)S(1)}, f32[2,1,32,512]{3,2,1,0:T(8,128)S(1)}, u32[]{:S(2)}, u32[]{:S(2)}) collective-permute-start(f32[2,1,32,512]{3,2,1,0:T(8,128)S(1)} %get-tuple-element.23), channel_id=1, source_target_pairs={{4,0},{8,4},{12,8},{5,1},{9,5},{13,9},{6,2},{10,6},{14,10},{7,3},{... | collective-permute-start | bytes 393224 | tf_op jit(solution)/shard_map/ppermute | solution.py:27
  30.3 3.8 %collective-permute-start.10 = (f32[2,4,1,512]{3,2,1,0:T(1,128)S(1)}, f32[2,4,1,512]{3,2,1,0:T(1,128)S(1)}, u32[]{:S(2)}, u32[]{:S(2)}) collective-permute-start(f32[2,4,1,512]{3,2,1,0:T(1,128)S(1)} %get-tuple-element.25), channel_id=1, source_target_pairs={{2,0},{0,2},{3,1},{1,3},{6,4},{4,6},{7,5},{5,7},{10,8},{8,10},{11,... | collective-permute-start | bytes 49160 | tf_op jit(solution)/shard_map/ppermute | solution.py:27
  31.9 3.7 %collective-permute-start.9 = (f32[2,4,1,512]{3,2,1,0:T(1,128)S(1)}, f32[2,4,1,512]{3,2,1,0:T(1,128)S(1)}, u32[]{:S(2)}, u32[]{:S(2)}) collective-permute-start(f32[2,4,1,512]{3,2,1,0:T(1,128)S(1)} %get-tuple-element.24), channel_id=1, source_target_pairs={{0,2},{2,0},{1,3},{3,1},{4,6},{6,4},{5,7},{7,5},{8,10},{10,8},{9,1... | collective-permute-start | bytes 49160 | tf_op jit(solution)/shard_map/ppermute | solution.py:26
  35.7 1.5 %collective-permute-start.11 = (f32[2,4,34,1]{3,2,1,0:T(8,128)S(1)}, f32[2,4,34,1]{3,2,1,0:T(8,128)S(1)}, u32[]{:S(2)}, u32[]{:S(2)}) collective-permute-start(f32[2,4,34,1]{3,2,1,0:T(8,128)S(1)} %get-tuple-element.10), channel_id=1, source_target_pairs={{0,1},{1,0},{2,3},{3,2},{4,5},{5,4},{6,7},{7,6},{8,9},{9,8},{10,11... | collective-permute-start | bytes 3272 | tf_op jit(solution)/shard_map/ppermute | solution.py:26
  35.8 1.6 %collective-permute-start.12 = (f32[2,4,34,1]{3,2,1,0:T(8,128)S(1)}, f32[2,4,34,1]{3,2,1,0:T(8,128)S(1)}, u32[]{:S(2)}, u32[]{:S(2)}) collective-permute-start(f32[2,4,34,1]{3,2,1,0:T(8,128)S(1)} %get-tuple-element.11), channel_id=1, source_target_pairs={{1,0},{0,1},{3,2},{2,3},{5,4},{4,5},{7,6},{6,7},{9,8},{8,9},{11,10... | collective-permute-start | bytes 3272 | tf_op jit(solution)/shard_map/ppermute | solution.py:27
  38.8 8.5 %collective-permute-start.13 = (f32[2,1,32,512]{3,2,1,0:T(8,128)S(1)}, f32[2,1,32,512]{3,2,1,0:T(8,128)S(1)}, u32[]{:S(2)}, u32[]{:S(2)}) collective-permute-start(f32[2,1,32,512]{3,2,1,0:T(8,128)S(1)} %fusion.96), channel_id=1, source_target_pairs={{4,0},{8,4},{12,8},{5,1},{9,5},{13,9},{6,2},{10,6},{14,10},{7,3},{... | collective-permute-start | bytes 393224 | tf_op jit(solution)/shard_map/ppermute | solution.py:35
  47.5 7.1 %collective-permute-start.16 = (f32[2,4,1,512]{3,2,1,0:T(1,128)S(1)}, f32[2,4,1,512]{3,2,1,0:T(1,128)S(1)}, u32[]{:S(2)}, u32[]{:S(2)}) collective-permute-start(f32[2,4,1,512]{3,2,1,0:T(1,128)S(1)} %get-tuple-element.19), channel_id=1, source_target_pairs={{0,2},{2,0},{1,3},{3,1},{4,6},{6,4},{5,7},{7,5},{8,10},{10,8},{9,1... | collective-permute-start | bytes 49160 | tf_op jit(solution)/shard_map/ppermute | solution.py:26
  48.1 6.5 %collective-permute-start.17 = (f32[2,4,1,512]{3,2,1,0:T(1,128)S(1)}, f32[2,4,1,512]{3,2,1,0:T(1,128)S(1)}, u32[]{:S(2)}, u32[]{:S(2)}) collective-permute-start(f32[2,4,1,512]{3,2,1,0:T(1,128)S(1)} %get-tuple-element.18), channel_id=1, source_target_pairs={{2,0},{0,2},{3,1},{1,3},{6,4},{4,6},{7,5},{5,7},{10,8},{8,10},{11,... | collective-permute-start | bytes 49160 | tf_op jit(solution)/shard_map/ppermute | solution.py:27
  49.6 6.1 %collective-permute-start.14 = (f32[2,1,32,512]{3,2,1,0:T(8,128)S(1)}, f32[2,1,32,512]{3,2,1,0:T(8,128)S(1)}, u32[]{:S(2)}, u32[]{:S(2)}) collective-permute-start(f32[2,1,32,512]{3,2,1,0:T(8,128)S(1)} %get-tuple-element.17), channel_id=1, source_target_pairs={{0,4},{4,8},{8,12},{1,5},{5,9},{9,13},{2,6},{6,10},{10,14},{3,7},{... | collective-permute-start | bytes 393224 | tf_op jit(solution)/shard_map/ppermute | solution.py:26
  53.2 6.9 %collective-permute-start.15 = (f32[2,1,32,512]{3,2,1,0:T(8,128)S(1)}, f32[2,1,32,512]{3,2,1,0:T(8,128)S(1)}, u32[]{:S(2)}, u32[]{:S(2)}) collective-permute-start(f32[2,1,32,512]{3,2,1,0:T(8,128)S(1)} %get-tuple-element.16), channel_id=1, source_target_pairs={{4,0},{8,4},{12,8},{5,1},{9,5},{13,9},{6,2},{10,6},{14,10},{7,3},{... | collective-permute-start | bytes 393224 | tf_op jit(solution)/shard_map/ppermute | solution.py:27
  54.7 5.4 %collective-permute-start.18 = (f32[2,4,34,1]{3,2,1,0:T(8,128)S(1)}, f32[2,4,34,1]{3,2,1,0:T(8,128)S(1)}, u32[]{:S(2)}, u32[]{:S(2)}) collective-permute-start(f32[2,4,34,1]{3,2,1,0:T(8,128)S(1)} %get-tuple-element.9), channel_id=1, source_target_pairs={{0,1},{1,0},{2,3},{3,2},{4,5},{5,4},{6,7},{7,6},{8,9},{9,8},{10,11... | collective-permute-start | bytes 3272 | tf_op jit(solution)/shard_map/ppermute | solution.py:26
  54.7 5.4 %collective-permute-start.19 = (f32[2,4,34,1]{3,2,1,0:T(8,128)S(1)}, f32[2,4,34,1]{3,2,1,0:T(8,128)S(1)}, u32[]{:S(2)}, u32[]{:S(2)}) collective-permute-start(f32[2,4,34,1]{3,2,1,0:T(8,128)S(1)} %get-tuple-element.8), channel_id=1, source_target_pairs={{1,0},{0,1},{3,2},{2,3},{5,4},{4,5},{7,6},{6,7},{9,8},{8,9},{11,10... | collective-permute-start | bytes 3272 | tf_op jit(solution)/shard_map/ppermute | solution.py:27
where the time goes:
time: 63.2 us; the launch traced here: 62.9 us
  starting transfers between devices  27 us (43%)
  waiting for transfers between devices  26.9 us (43%)
  other arithmetic  7.19 us (11%)
  between operations  1.67 us (3%)
    ppermute x9, starting transfers between devices, extended(): before = lax.ppermute(last, axis, up)  15.4 us
    ppermute x2, waiting for transfers between devices, passed_along(): return lax.ppermute(shard, axis, pairs)  12.6 us
    ppermute x9, waiting for transfers between devices, extended(): after = lax.ppermute(first, axis, down)  11.5 us
    ppermute x9, starting transfers between devices, extended(): after = lax.ppermute(first, axis, down)  8.95 us
    ppermute x9, waiting for transfers between devices, extended(): before = lax.ppermute(last, axis, up)  2.79 us
    add x2, other arithmetic, advance(): solutes + time_step * solute_rate  2.72 us
    ppermute x2, starting transfers between devices, passed_along(): return lax.ppermute(shard, axis, pairs)  2.58 us
    another operation x6, other arithmetic, advance(): jnp.stack([phases + time_step * growth_rate, solutes + time_step * solute...  1.39 us
  transfers between devices with their start and end apart: 20, of which 10 were waited for; matrix products, arithmetic and copies ran while one was open for 1% of the time, Pallas kernels for 0%

commit v1 on v0

v1 whole, which is shorter than its diff:
```python
import functools

import jax
import jax.numpy as jnp
from jax import lax
from jax.experimental import pallas as pl
from jax.experimental.pallas import tpu as pltpu
from jax.sharding import PartitionSpec as P

partition = 0.15
coupling = 2.0
diffusion = 2.0
spacing_sq = 0.64
time_step = 0.025
gradient_scale = 1.2
drift_rate = 0.01
seed_levels = 1024.0

MESH = pl.DeviceIdType.MESH
EDGE = 4
COL = 128
FIRST = 2


def kernel(sizes, shift_ref, seed_ref, phi_in, sol_in, phi_out, sol_out,
           start, col_next, col_prev, one, two,
           local_sem, z_send, z_recv, y0_send, y0_recv, y_send, y_recv, x_send, x_recv):
    planes, rows, lanes = sizes
    inputs = (phi_in, sol_in)
    gi = lax.axis_index("grow")
    g_last = lax.axis_size("grow") - 1
    ci, c_n = lax.axis_index("cross"), lax.axis_size("cross")
    si, s_n = lax.axis_index("side"), lax.axis_size("side")
    c_next, c_prev = lax.rem(ci + 1, c_n), lax.rem(ci + c_n - 1, c_n)
    s_next, s_prev = lax.rem(si + 1, s_n), lax.rem(si + s_n - 1, s_n)
    at_bottom, at_top = gi == 0, gi == g_last
    inside = (pl.ds(0, rows), pl.ds(0, lanes))

    def remote(src, dst, send, recv, **where):
        return pltpu.make_async_remote_copy(src_ref=src, dst_ref=dst, send_sem=send, recv_sem=recv,
                                            device_id=where, device_id_type=MESH)

    def z_down(field, plane):
        n = 2 * plane + field
        return remote(inputs[field].at[plane], start.at[(field, FIRST + planes + plane) + inside],
                      z_send.at[n], z_recv.at[n], grow=gi - 1)

    def z_up(field, k):
        n = 2 * (planes + k) + field
        return remote(inputs[field].at[planes - 1 - k], start.at[(field, FIRST - 1 - k) + inside],
                      z_send.at[n], z_recv.at[n], grow=gi + 1)

    def y_own(field):
        own = pl.ds(FIRST, planes)
        low = remote(inputs[field].at[:, pl.ds(0, EDGE), :],
                     start.at[field, own, pl.ds(rows, EDGE), pl.ds(0, lanes)],
                     y0_send.at[2 * field], y0_recv.at[2 * field], cross=c_prev)
        high = remote(inputs[field].at[:, pl.ds(rows - EDGE, EDGE), :],
                      start.at[field, own, pl.ds(rows + EDGE, EDGE), pl.ds(0, lanes)],
                      y0_send.at[2 * field + 1], y0_recv.at[2 * field + 1], cross=c_next)
        return low, high

    def y_relay(group, slot):
        low = remote(start.at[:, slot, pl.ds(0, EDGE), pl.ds(0, lanes)],
                     start.at[:, slot, pl.ds(rows, EDGE), pl.ds(0, lanes)],
                     y_send.at[2 * group], y_recv.at[2 * group], cross=c_prev)
        high = remote(start.at[:, slot, pl.ds(rows - EDGE, EDGE), pl.ds(0, lanes)],
                      start.at[:, slot, pl.ds(rows + EDGE, EDGE), pl.ds(0, lanes)],
                      y_send.at[2 * group + 1], y_recv.at[2 * group + 1], cross=c_next)
        return low, high

    def x_copies(group, slot, count):
        own = pl.ds(slot, count)
        low = remote(start.at[:, own, :, pl.ds(0, COL)], col_next.at[:, own],
                     x_send.at[2 * group], x_recv.at[2 * group], side=s_prev)
        high = remote(start.at[:, own, :, pl.ds(lanes - COL, COL)], col_prev.at[:, own],
                      x_send.at[2 * group + 1], x_recv.at[2 * group + 1], side=s_next)
        return low, high

    def combine(slot, count):
        near = lax.broadcasted_iota(jnp.int32, (rows + 2 * EDGE, COL), 1) < COL // 2
        for s in range(slot, slot + count):
            for f in range(2):
                start[f, s, :, pl.ds(lanes, COL)] = jnp.where(near, col_next[f, s], col_prev[f, s])

    wide, tall = lanes + COL, rows + 2 * EDGE
    grid_rows = planes * lax.axis_size("grow")

    def flux(w, u, wn, un):
        return (w + wn) * (un - u)

    def hole(phases):
        return 1.0 - jnp.clip(phases, -1.0, 1.0)

    def advance(center, lower, upper, plane, step):
        p, u = center
        height = (gi * planes + plane).astype(jnp.float32)
        temper = gradient_scale * ((height + 0.5) / grid_rows - 0.5) - drift_rate * step
        w = hole(p)
        total = lower[0] + upper[0]
        flow = flux(w, u, hole(lower[0]), lower[1]) + flux(w, u, hole(upper[0]), upper[1])
        for axis, size in ((0, tall), (1, wide)):
            pn, un = pltpu.roll(p, size - 1, axis), pltpu.roll(u, size - 1, axis)
            total = total + pn + pltpu.roll(p, 1, axis)
            f = flux(w, u, hole(pn), un)
            flow = flow + f - pltpu.roll(f, 1, axis)
        laplace = (total - 6.0 * p) * (1.0 / spacing_sq)
        room = 1.0 - p * p
        driving = laplace + p * room - coupling * (room * room) * (u + temper)
        slowing = 1.0 - (1.0 - partition) * temper
        change = driving * (time_step / jnp.full((1, wide), slowing, jnp.float32))
        gain = flow * (0.5 * time_step * diffusion / spacing_sq) + (1.0 + (1.0 - partition) * u) * change
        weight = 2.0 * partition + (1.0 - partition) * w
        return p + change, u + gain / weight

    def pick(cond, a, b):
        return tuple(jnp.where(cond, x, y) for x, y in zip(a, b))

    def t0(k):
        return start[0, FIRST + k], start[1, FIRST + k]

    def t1(k):
        return one[0, 1 + k], one[1, 1 + k]

    def t2(k):
        return two[0, k], two[1, k]

    def put1(k, v):
        one[0, 1 + k], one[1, 1 + k] = v

    def put2(k, v):
        two[0, k], two[1, k] = v

    moved_early = shift_ref[0] == 0
    last = planes

    def step0(k):
        lower, upper = t0(k - 1), t0(k + 1)
        if k == 0:
            lower = pick(at_bottom, t0(0), lower)
        if k == last - 1:
            upper = pick(at_top, t0(k), upper)
        put1(k, advance(t0(k), lower, upper, k, 0))

    def step1(k):
        put2(k, advance(t1(k), t1(k - 1), t1(k + 1), k, 1))

    def step2(k):
        a, b = advance(t2(k), t2(k - 1), t2(k + 1), k, 2)
        phi_out[k - 1] = a[:rows, :lanes]
        sol_out[k - 1] = b[:rows, :lanes]

    @pl.when(at_top)
    def _():
        start[(0, FIRST + planes) + inside] = jnp.full((rows, lanes), -1.0, jnp.float32)
        start[(1, FIRST + planes) + inside] = seed_ref[...].astype(jnp.float32) / seed_levels - 1.0

    own_copies = [pltpu.make_async_copy(inputs[f], start.at[(f, pl.ds(FIRST, planes)) + inside], local_sem.at[f])
                  for f in range(2)]
    for copy in own_copies:
        copy.start()

    barrier = pltpu.get_barrier_semaphore()
    for where in (dict(cross=c_next), dict(cross=c_prev), dict(side=s_next), dict(side=s_prev)):
        pl.semaphore_signal(barrier, inc=1, device_id=where, device_id_type=MESH)

    @pl.when(jnp.logical_not(at_bottom))
    def _():
        pl.semaphore_signal(barrier, inc=1, device_id=dict(grow=gi - 1), device_id_type=MESH)

    @pl.when(jnp.logical_not(at_top))
    def _():
        pl.semaphore_signal(barrier, inc=1, device_id=dict(grow=gi + 1), device_id_type=MESH)

    ends = at_bottom.astype(jnp.int32) + at_top.astype(jnp.int32)
    pl.semaphore_wait(barrier, 6 - ends)

    fields = range(2)
    has_lower, has_upper = jnp.logical_not(at_bottom), jnp.logical_not(at_top)

    @pl.when(has_lower)
    def _():
        for plane in range(planes):
            for f in fields:
                z_down(f, plane).start()

    @pl.when(has_upper)
    def _():
        for k in range(2):
            for f in fields:
                z_up(f, k).start()

    own_y = [c for f in fields for c in y_own(f)]
    for c in own_y:
        c.start()
    for copy in own_copies:
        copy.wait()
    for c in own_y:
        c.wait_recv()
    own_x = x_copies(0, FIRST, planes)
    for c in own_x:
        c.start()

    below, above = FIRST - 1, FIRST + planes

    def start_y(group, slot):
        for c in y_relay(group, slot):
            c.start()

    def pass_x(group, slot):
        for c in y_relay(group, slot):
            c.wait_recv()
        for c in x_copies(group + 1, slot, 1):
            c.start()

    def finish_x(group, slot):
        for c in x_copies(group + 1, slot, 1):
            c.wait_recv()
        combine(slot, 1)

    for c in own_x:
        c.wait_recv()
    combine(FIRST, planes)
    step0(1)
    step0(2)

    @pl.when(has_lower)
    def _():
        for f in fields:
            z_up(f, 0).wait_recv()
        start_y(0, below)

    @pl.when(has_upper)
    def _():
        for f in fields:
            z_down(f, 0).wait_recv()

    start_y(1, above)

    @pl.when(has_lower)
    def _():
        pass_x(0, below)

    pass_x(1, above)

    @pl.when(has_lower)
    def _():
        finish_x(0, below)

    finish_x(1, above)
    step0(0)
    step0(3)
    put1(0, pick(jnp.logical_and(at_bottom, moved_early), t1(1), t1(0)))
    step1(1)
    step1(2)

    @pl.when(has_upper)
    def _():
        for f in fields:
            z_down(f, 1).wait_recv()
        start_y(2, above + 1)

    @pl.when(has_lower)
    def _():
        for f in fields:
            z_up(f, 1).wait_recv()

    step0(-1)
    put1(-1, pick(at_bottom, t1(0), t1(-1)))
    step1(0)
    put2(0, pick(at_bottom, t2(1), t2(0)))
    step2(1)

    @pl.when(has_upper)
    def _():
        pass_x(2, above + 1)
        finish_x(2, above + 1)

    step0(4)
    put1(4, pick(at_top, pick(moved_early, t0(4), t1(3)), t1(4)))
    step1(3)
    step2(2)

    @pl.when(has_upper)
    def _():
        for f in fields:
            z_down(f, 2).wait_recv()
        start_y(3, above + 2)
        pass_x(3, above + 2)
        finish_x(3, above + 2)

    step0(5)
    put1(5, pick(at_top, t1(4), t1(5)))
    step1(4)
    put2(4, pick(jnp.logical_and(at_top, jnp.logical_not(moved_early)), t0(4), t2(4)))
    step2(3)

    @pl.when(has_upper)
    def _():
        for f in fields:
            z_down(f, 3).wait_recv()

    step0(6)
    step1(5)
    put2(5, pick(at_top, t2(4), t2(5)))
    step2(4)

    for c in own_y + list(own_x):
        c.wait_send()
    for c in y_relay(1, above) + x_copies(2, above, 1):
        c.wait_send()

    @pl.when(has_lower)
    def _():
        for plane in range(planes):
            for f in fields:
                z_down(f, plane).wait_send()
        for c in y_relay(0, below) + x_copies(1, below, 1):
            c.wait_send()

    @pl.when(has_upper)
    def _():
        for k in range(2):
            for f in fields:
                z_up(f, k).wait_send()
        for g in (2, 3):
            for c in y_relay(g, above + g - 1) + x_copies(g + 1, above + g - 1, 1):
                c.wait_send()


def shards(phase_field, solute_field, shift_step, inflow_seed):
    planes, rows, lanes = phase_field.shape
    tall, wide = rows + 2 * EDGE, lanes + COL
    field = jax.ShapeDtypeStruct(phase_field.shape, jnp.float32)
    dma = pltpu.SemaphoreType.DMA
    vmem, hbm = pl.BlockSpec(memory_space=pltpu.VMEM), pl.BlockSpec(memory_space=pl.ANY)
    slots = 2 * planes + 2
    return pl.pallas_call(
        functools.partial(kernel, (planes, rows, lanes)),
        out_shape=(field, field),
        in_specs=[pl.BlockSpec(memory_space=pltpu.SMEM), vmem, hbm, hbm],
        out_specs=(vmem, vmem),
        scratch_shapes=[
            pltpu.VMEM((2, slots, tall, wide), jnp.float32),
            pltpu.VMEM((2, slots, tall, COL), jnp.float32),
            pltpu.VMEM((2, slots, tall, COL), jnp.float32),
            pltpu.VMEM((2, planes + 4, tall, wide), jnp.float32),
            pltpu.VMEM((2, planes + 2, tall, wide), jnp.float32),
            dma((2,)), dma((2 * (planes + 2),)), dma((2 * (planes + 2),)),
            dma((4,)), dma((4,)), dma((8,)), dma((8,)), dma((10,)), dma((10,)),
        ],
        compiler_params=pltpu.CompilerParams(collective_id=0, has_side_effects=True),
    )(shift_step, inflow_seed, phase_field, solute_field)


def solution(mesh):
    return jax.shard_map(
        shards,
        mesh=mesh,
        in_specs=(
            P(("groups", "grow"), "cross", "side"),
            P(("groups", "grow"), "cross", "side"),
            P("groups"),
            P(("groups", "cross"), "side"),
        ),
        out_specs=(P(("groups", "grow"), "cross", "side"), P(("groups", "grow"), "cross", "side")),
        check_vma=False,
    )
```

time: 63.2 us -> 29.7 us (0.47)
  the two profiles are of different devices: /device:TPU:0 before, /device:TPU:1 now
where the time goes in v1:
time: 29.7 us; the launch traced here: 29.5 us
  Pallas kernels  25.8 us (87%)
  local copies, waits for them, and re-layouts  2.42 us (8%)
  between operations  1.29 us (4%)
    pallas_call x1, Pallas kernels, shards(): pl.pallas_call(functools.partial(kernel, (planes, rows, lanes)), out_shap...  25.8 us
    unnamed x4, local copies, waits for them, and re-layouts  2.42 us

profile of v1, /device:TPU:1, one launch (start us, length us, event | category | flops | bytes accessed | tf_op | source)
XLA Modules:
  0.0 29.5 jit_solution(4744496261484431157)
XLA Ops:
  1.3 25.8 %shard_map.59 = (f32[4,32,512]{2,1,0:T(8,128)}, f32[4,32,512]{2,1,0:T(8,128)}) custom-call(s32[1]{0:T(128)S(6)} %copy.8.shift_ref, s32[32,512]{1,0:T(8,128)} %seed_ref.1, f32[4,32,512]{2,1,0:T(8,128)} %phi_in.1, f32[4,32,512]{2,1,0:T(8,128)} %sol_in.1), custom_call_target="tpu_custom_call" | custom-call | tf_op jit(solution)/shard_map/pallas_call | solution.py:338
  27.1 0.0 copy-start
  27.1 1.7 %copy.9 = f32[4,32,512]{2,1,0:T(8,128)} copy(f32[4,32,512]{2,1,0:T(8,128)} %get-tuple-element.4) | data formatting | bytes 524288
  28.8 0.0 copy-done
  28.8 0.7 %copy.10 = f32[4,32,512]{2,1,0:T(8,128)} copy(f32[4,32,512]{2,1,0:T(8,128)S(1)} %copy-done) | data formatting | bytes 524288
Async XLA Ops:
  27.1 1.7 %copy-start = (f32[4,32,512]{2,1,0:T(8,128)S(1)}, f32[4,32,512]{2,1,0:T(8,128)}, u32[]{:S(2)}) copy-start(f32[4,32,512]{2,1,0:T(8,128)} %get-tuple-element.5) | copy-start | bytes 786436

commit v2 on v1

--- a/solution.py
+++ b/solution.py
@@ -23,8 +23,8 @@
 
 
 def kernel(sizes, shift_ref, seed_ref, phi_in, sol_in, phi_out, sol_out,
-           start, col_next, col_prev, one, two,
-           local_sem, z_send, z_recv, y0_send, y0_recv, y_send, y_recv, x_send, x_recv):
+           start, col_next, col_prev, one, two, seed_vmem,
+           local_sem, diag_send, diag_recv, z_send, z_recv, y0_send, y0_recv, y_send, y_recv, x_send, x_recv):
     planes, rows, lanes = sizes
     inputs = (phi_in, sol_in)
     gi = lax.axis_index("grow")
@@ -33,6 +33,7 @@
     si, s_n = lax.axis_index("side"), lax.axis_size("side")
     c_next, c_prev = lax.rem(ci + 1, c_n), lax.rem(ci + c_n - 1, c_n)
     s_next, s_prev = lax.rem(si + 1, s_n), lax.rem(si + s_n - 1, s_n)
+    wide, tall = lanes + COL, rows + 2 * EDGE
     at_bottom, at_top = gi == 0, gi == g_last
     inside = (pl.ds(0, rows), pl.ds(0, lanes))
 
@@ -50,24 +51,27 @@
         return remote(inputs[field].at[planes - 1 - k], start.at[(field, FIRST - 1 - k) + inside],
                       z_send.at[n], z_recv.at[n], grow=gi + 1)
 
+    def y_pair(src_of, dst_of, count, send, recv, first, **where):
+        low = remote(src_of(pl.ds(0, count)), dst_of(pl.ds(rows, count)),
+                     send.at[first], recv.at[first], cross=c_prev, **where)
+        high = remote(src_of(pl.ds(rows - count, count)), dst_of(pl.ds(tall - count, count)),
+                      send.at[first + 1], recv.at[first + 1], cross=c_next, **where)
+        return low, high
+
     def y_own(field):
-        own = pl.ds(FIRST, planes)
-        low = remote(inputs[field].at[:, pl.ds(0, EDGE), :],
-                     start.at[field, own, pl.ds(rows, EDGE), pl.ds(0, lanes)],
-                     y0_send.at[2 * field], y0_recv.at[2 * field], cross=c_prev)
-        high = remote(inputs[field].at[:, pl.ds(rows - EDGE, EDGE), :],
-                      start.at[field, own, pl.ds(rows + EDGE, EDGE), pl.ds(0, lanes)],
-                      y0_send.at[2 * field + 1], y0_recv.at[2 * field + 1], cross=c_next)
-        return low, high
+        return y_pair(lambda r: inputs[field].at[:, r, :],
+                      lambda r: start.at[field, pl.ds(FIRST, planes), r, pl.ds(0, lanes)],
+                      3, y0_send, y0_recv, 2 * field)
 
     def y_relay(group, slot):
-        low = remote(start.at[:, slot, pl.ds(0, EDGE), pl.ds(0, lanes)],
-                     start.at[:, slot, pl.ds(rows, EDGE), pl.ds(0, lanes)],
-                     y_send.at[2 * group], y_recv.at[2 * group], cross=c_prev)
-        high = remote(start.at[:, slot, pl.ds(rows - EDGE, EDGE), pl.ds(0, lanes)],
-                      start.at[:, slot, pl.ds(rows + EDGE, EDGE), pl.ds(0, lanes)],
-                      y_send.at[2 * group + 1], y_recv.at[2 * group + 1], cross=c_next)
-        return low, high
+        view = lambda r: start.at[:, slot, r, pl.ds(0, lanes)]
+        return y_pair(view, view, (1, 3, 2)[group], y_send, y_recv, 2 * group)
+
+    def y_diag(field):
+        plane = planes - 2
+        return y_pair(lambda r: inputs[field].at[plane, r, :],
+                      lambda r: start.at[field, FIRST + planes + plane, r, pl.ds(0, lanes)],
+                      1, diag_send, diag_recv, 2 * field, grow=gi - 1)
 
     def x_copies(group, slot, count):
         own = pl.ds(slot, count)
@@ -83,7 +87,6 @@
             for f in range(2):
                 start[f, s, :, pl.ds(lanes, COL)] = jnp.where(near, col_next[f, s], col_prev[f, s])
 
-    wide, tall = lanes + COL, rows + 2 * EDGE
     grid_rows = planes * lax.axis_size("grow")
 
     def flux(w, u, wn, un):
@@ -131,7 +134,6 @@
     def put2(k, v):
         two[0, k], two[1, k] = v
 
-    moved_early = shift_ref[0] == 0
     last = planes
 
     def step0(k):
@@ -150,30 +152,31 @@
         phi_out[k - 1] = a[:rows, :lanes]
         sol_out[k - 1] = b[:rows, :lanes]
 
-    @pl.when(at_top)
-    def _():
-        start[(0, FIRST + planes) + inside] = jnp.full((rows, lanes), -1.0, jnp.float32)
-        start[(1, FIRST + planes) + inside] = seed_ref[...].astype(jnp.float32) / seed_levels - 1.0
-
     own_copies = [pltpu.make_async_copy(inputs[f], start.at[(f, pl.ds(FIRST, planes)) + inside], local_sem.at[f])
                   for f in range(2)]
     for copy in own_copies:
         copy.start()
 
+    @pl.when(at_top)
+    def _():
+        seeds = pltpu.make_async_copy(seed_ref, seed_vmem, local_sem.at[2])
+        seeds.start()
+        seeds.wait()
+        start[(0, FIRST + planes) + inside] = jnp.full((rows, lanes), -1.0, jnp.float32)
+        start[(1, FIRST + planes) + inside] = seed_vmem[...].astype(jnp.float32) / seed_levels - 1.0
+
     barrier = pltpu.get_barrier_semaphore()
     for where in (dict(cross=c_next), dict(cross=c_prev), dict(side=s_next), dict(side=s_prev)):
         pl.semaphore_signal(barrier, inc=1, device_id=where, device_id_type=MESH)
 
-    @pl.when(jnp.logical_not(at_bottom))
-    def _():
-        pl.semaphore_signal(barrier, inc=1, device_id=dict(grow=gi - 1), device_id_type=MESH)
-
-    @pl.when(jnp.logical_not(at_top))
-    def _():
-        pl.semaphore_signal(barrier, inc=1, device_id=dict(grow=gi + 1), device_id_type=MESH)
+    for edge, near in ((at_bottom, gi - 1), (at_top, gi + 1)):
+        @pl.when(jnp.logical_not(edge))
+        def _():
+            for where in (dict(grow=near), dict(grow=near, cross=c_next), dict(grow=near, cross=c_prev)):
+                pl.semaphore_signal(barrier, inc=1, device_id=where, device_id_type=MESH)
 
     ends = at_bottom.astype(jnp.int32) + at_top.astype(jnp.int32)
-    pl.semaphore_wait(barrier, 6 - ends)
+    pl.semaphore_wait(barrier, 10 - 3 * ends)
 
     fields = range(2)
     has_lower, has_upper = jnp.logical_not(at_bottom), jnp.logical_not(at_top)
@@ -183,6 +186,10 @@
         for plane in range(planes):
             for f in fields:
                 z_down(f, plane).start()
+            if plane == 0:
+                for f in fields:
+                    for c in y_diag(f):
+                        c.start()
 
     @pl.when(has_upper)
     def _():
@@ -218,6 +225,20 @@
             c.wait_recv()
         combine(slot, 1)
 
+    moved_early = shift_ref[0] == 0
+
+    @pl.when(has_lower)
+    def _():
+        for f in fields:
+            z_up(f, 0).wait_recv()
+        start_y(0, below)
+
+    @pl.when(has_upper)
+    def _():
+        for f in fields:
+            z_down(f, 0).wait_recv()
+
+    start_y(1, above)
     for c in own_x:
         c.wait_recv()
     combine(FIRST, planes)
@@ -226,22 +247,15 @@
 
     @pl.when(has_lower)
     def _():
-        for f in fields:
-            z_up(f, 0).wait_recv()
-        start_y(0, below)
-
-    @pl.when(has_upper)
-    def _():
-        for f in fields:
-            z_down(f, 0).wait_recv()
-
-    start_y(1, above)
-
-    @pl.when(has_lower)
-    def _():
         pass_x(0, below)
 
     pass_x(1, above)
+
+    @pl.when(has_upper)
+    def _():
+        for f in fields:
+            z_down(f, 1).wait_recv()
+        start_y(2, above + 1)
 
     @pl.when(has_lower)
     def _():
@@ -254,12 +268,6 @@
     step1(1)
     step1(2)
 
-    @pl.when(has_upper)
-    def _():
-        for f in fields:
-            z_down(f, 1).wait_recv()
-        start_y(2, above + 1)
-
     @pl.when(has_lower)
     def _():
         for f in fields:
@@ -274,6 +282,12 @@
     @pl.when(has_upper)
     def _():
         pass_x(2, above + 1)
+        for f in fields:
+            z_down(f, 2).wait_recv()
+            for c in y_diag(f):
+                c.wait_recv()
+        for c in x_copies(4, above + 2, 1):
+            c.start()
         finish_x(2, above + 1)
 
     step0(4)
@@ -283,10 +297,6 @@
 
     @pl.when(has_upper)
     def _():
-        for f in fields:
-            z_down(f, 2).wait_recv()
-        start_y(3, above + 2)
-        pass_x(3, above + 2)
         finish_x(3, above + 2)
 
     step0(5)
@@ -315,6 +325,9 @@
         for plane in range(planes):
             for f in fields:
                 z_down(f, plane).wait_send()
+        for f in fields:
+            for c in y_diag(f):
+                c.wait_send()
         for c in y_relay(0, below) + x_copies(1, below, 1):
             c.wait_send()
 
@@ -323,9 +336,8 @@
         for k in range(2):
             for f in fields:
                 z_up(f, k).wait_send()
-        for g in (2, 3):
-            for c in y_relay(g, above + g - 1) + x_copies(g + 1, above + g - 1, 1):
-                c.wait_send()
+        for c in y_relay(2, above + 1) + x_copies(3, above + 1, 1) + x_copies(4, above + 2, 1):
+            c.wait_send()
 
 
 def shards(phase_field, solute_field, shift_step, inflow_seed):
@@ -335,10 +347,11 @@
     dma = pltpu.SemaphoreType.DMA
     vmem, hbm = pl.BlockSpec(memory_space=pltpu.VMEM), pl.BlockSpec(memory_space=pl.ANY)
     slots = 2 * planes + 2
+    on_chip = pltpu.VMEM(phase_field.shape, jnp.float32)
     return pl.pallas_call(
         functools.partial(kernel, (planes, rows, lanes)),
-        out_shape=(field, field),
-        in_specs=[pl.BlockSpec(memory_space=pltpu.SMEM), vmem, hbm, hbm],
+        out_shape=(on_chip, on_chip),
+        in_specs=[pl.BlockSpec(memory_space=pltpu.SMEM), hbm, hbm, hbm],
         out_specs=(vmem, vmem),
         scratch_shapes=[
             pltpu.VMEM((2, slots, tall, wide), jnp.float32),
@@ -346,8 +359,9 @@
             pltpu.VMEM((2, slots, tall, COL), jnp.float32),
             pltpu.VMEM((2, planes + 4, tall, wide), jnp.float32),
             pltpu.VMEM((2, planes + 2, tall, wide), jnp.float32),
-            dma((2,)), dma((2 * (planes + 2),)), dma((2 * (planes + 2),)),
-            dma((4,)), dma((4,)), dma((8,)), dma((8,)), dma((10,)), dma((10,)),
+            pltpu.VMEM((rows, lanes), jnp.int32),
+            dma((3,)), dma((4,)), dma((4,)), dma((2 * (planes + 2),)), dma((2 * (planes + 2),)),
+            dma((4,)), dma((4,)), dma((6,)), dma((6,)), dma((10,)), dma((10,)),
         ],
         compiler_params=pltpu.CompilerParams(collective_id=0, has_side_effects=True),
     )(shift_step, inflow_seed, phase_field, solute_field)

time: 29.7 us -> 22.3 us (0.75)
  Pallas kernels: 25.8 us -> 19.3 us
  local copies, waits for them, and re-layouts: 2.42 us -> 1.41 us
    pallas_call x1, Pallas kernels: 25.8 us -> 19.3 us  [shards(): pl.pallas_call(functools.partial(kernel, (planes, rows, lanes)), out_shap...]
    unnamed x4 -> x2, local copies, waits for them, and re-layouts: 2.42 us -> 1.41 us
where the time goes in v2:
time: 22.3 us; the launch traced here: 22 us
  Pallas kernels  19.3 us (87%)
  local copies, waits for them, and re-layouts  1.41 us (6%)
  between operations  1.28 us (6%)
    pallas_call x1, Pallas kernels, shards(): pl.pallas_call(functools.partial(kernel, (planes, rows, lanes)), out_shap...  19.3 us
    unnamed x2, local copies, waits for them, and re-layouts  1.41 us

profile of v2, /device:TPU:1, one launch (start us, length us, event | category | flops | bytes accessed | tf_op | source)
XLA Modules:
  0.0 22.0 jit_solution(10611409850962154276)
XLA Ops:
  1.3 19.3 %shard_map.59 = (f32[4,32,512]{2,1,0:T(8,128)S(1)}, f32[4,32,512]{2,1,0:T(8,128)S(1)}) custom-call(s32[1]{0:T(128)S(6)} %copy.10.shift_ref, s32[32,512]{1,0:T(8,128)} %seed_ref.1, f32[4,32,512]{2,1,0:T(8,128)} %phi_in.1, f32[4,32,512]{2,1,0:T(8,128)} %sol_in.1), custom_call_target="tpu_custom_call" | custom-call | tf_op jit(solution)/shard_map/pallas_call | solution.py:351
  20.6 0.7 %copy.8 = f32[4,32,512]{2,1,0:T(8,128)} copy(f32[4,32,512]{2,1,0:T(8,128)S(1)} %get-tuple-element.2) | data formatting | bytes 524288
  21.3 0.7 %copy.9 = f32[4,32,512]{2,1,0:T(8,128)} copy(f32[4,32,512]{2,1,0:T(8,128)S(1)} %get-tuple-element.3) | data formatting | bytes 524288

commit v3 on v2

--- a/solution.py
+++ b/solution.py
@@ -340,6 +340,14 @@
             c.wait_send()
 
 
+def write_out(phi_ref, sol_ref, phi_out, sol_out, sem):
+    copies = [pltpu.make_async_copy(phi_ref, phi_out, sem.at[0]), pltpu.make_async_copy(sol_ref, sol_out, sem.at[1])]
+    for copy in copies:
+        copy.start()
+    for copy in copies:
+        copy.wait()
+
+
 def shards(phase_field, solute_field, shift_step, inflow_seed):
     planes, rows, lanes = phase_field.shape
     tall, wide = rows + 2 * EDGE, lanes + COL
@@ -348,7 +356,7 @@
     vmem, hbm = pl.BlockSpec(memory_space=pltpu.VMEM), pl.BlockSpec(memory_space=pl.ANY)
     slots = 2 * planes + 2
     on_chip = pltpu.VMEM(phase_field.shape, jnp.float32)
-    return pl.pallas_call(
+    results = pl.pallas_call(
         functools.partial(kernel, (planes, rows, lanes)),
         out_shape=(on_chip, on_chip),
         in_specs=[pl.BlockSpec(memory_space=pltpu.SMEM), hbm, hbm, hbm],
@@ -365,6 +373,13 @@
         ],
         compiler_params=pltpu.CompilerParams(collective_id=0, has_side_effects=True),
     )(shift_step, inflow_seed, phase_field, solute_field)
+    return pl.pallas_call(
+        write_out,
+        out_shape=(field, field),
+        in_specs=[vmem, vmem],
+        out_specs=(hbm, hbm),
+        scratch_shapes=[dma((2,))],
+    )(*(pltpu.with_memory_space_constraint(x, pltpu.VMEM) for x in results))
 
 
 def solution(mesh):

time: 22.3 us -> 21.7 us (0.973)
  local copies, waits for them, and re-layouts: 1.41 us -> 0 us
  Pallas kernels: 19.3 us -> 20.1 us
    unnamed x2 -> x0, local copies, waits for them, and re-layouts: 1.41 us -> none
    pallas_call x0 -> x1, Pallas kernels: none -> 0.81 us  [shards(): pl.pallas_call(write_out, out_shape=(field, field), in_specs=[vmem, vmem]...]
where the time goes in v3:
time: 21.7 us; the launch traced here: 21.4 us
  Pallas kernels  20.1 us (93%)
  between operations  1.28 us (6%)
    pallas_call x1, Pallas kernels, shards(): pl.pallas_call(functools.partial(kernel, (planes, rows, lanes)), out_shap...  19.3 us
    pallas_call x1, Pallas kernels, shards(): pl.pallas_call(write_out, out_shape=(field, field), in_specs=[vmem, vmem]...  0.81 us

profile of v3, /device:TPU:1, one launch (start us, length us, event | category | flops | bytes accessed | tf_op | source)
XLA Modules:
  0.0 21.4 jit_solution(14668478804365703443)
XLA Ops:
  1.3 19.3 %shard_map.59 = (f32[4,32,512]{2,1,0:T(8,128)S(1)}, f32[4,32,512]{2,1,0:T(8,128)S(1)}) custom-call(s32[1]{0:T(128)S(6)} %copy.6.shift_ref, s32[32,512]{1,0:T(8,128)} %seed_ref.1, f32[4,32,512]{2,1,0:T(8,128)} %phi_in.1, f32[4,32,512]{2,1,0:T(8,128)} %sol_in.1), custom_call_target="tpu_custom_call" | custom-call | tf_op jit(solution)/shard_map/pallas_call | solution.py:359
  20.6 0.8 %shard_map.60 = (f32[4,32,512]{2,1,0:T(8,128)}, f32[4,32,512]{2,1,0:T(8,128)}) custom-call(f32[4,32,512]{2,1,0:T(8,128)S(1)} %get-tuple-element.4.phi_ref, f32[4,32,512]{2,1,0:T(8,128)S(1)} %get-tuple-element.5.sol_ref), custom_call_target="tpu_custom_call" | custom-call | tf_op jit(solution)/shard_map/pallas_call | solution.py:376

commit v4 on v3

--- a/solution.py
+++ b/solution.py
@@ -18,13 +18,14 @@
 
 MESH = pl.DeviceIdType.MESH
 EDGE = 4
+TILE = 8
 COL = 128
 FIRST = 2
 
 
 def kernel(sizes, shift_ref, seed_ref, phi_in, sol_in, phi_out, sol_out,
-           start, col_next, col_prev, one, two, seed_vmem,
-           local_sem, diag_send, diag_recv, z_send, z_recv, y0_send, y0_recv, y_send, y_recv, x_send, x_recv):
+           start, col_next, col_prev, one, two, edges, seed_vmem,
+           local_sem, edge_send, edge_recv, last_send, last_recv, z_send, z_recv, y0_send, y0_recv, y_send, y_recv, x_send, x_recv):
     planes, rows, lanes = sizes
     inputs = (phi_in, sol_in)
     gi = lax.axis_index("grow")
@@ -67,11 +68,23 @@
         view = lambda r: start.at[:, slot, r, pl.ds(0, lanes)]
         return y_pair(view, view, (1, 3, 2)[group], y_send, y_recv, 2 * group)
 
-    def y_diag(field):
-        plane = planes - 2
-        return y_pair(lambda r: inputs[field].at[plane, r, :],
-                      lambda r: start.at[field, FIRST + planes + plane, r, pl.ds(0, lanes)],
-                      1, diag_send, diag_recv, 2 * field, grow=gi - 1)
+    def z_edge(field):
+        plane = inputs[field].at[planes - 2]
+        return [remote(plane.at[pl.ds(row, 1), :], edges.at[field, side, pl.ds(0, 1), :],
+                       edge_send.at[2 * field + side], edge_recv.at[2 * field + side], grow=gi - 1)
+                for side, row in ((0, 0), (1, rows - 1))]
+
+    def y_edge(side):
+        row, where = ((rows, c_prev), (tall - 1, c_next))[side]
+        return remote(edges.at[:, side, pl.ds(0, 1), :],
+                      start.at[:, FIRST + 2 * planes - 2, pl.ds(row, 1), pl.ds(0, lanes)],
+                      edge_send.at[4 + side], edge_recv.at[4 + side], cross=where)
+
+    def z_last(field, r):
+        part = pl.ds(TILE * r, TILE)
+        return remote(inputs[field].at[planes - 1, part, :],
+                      start.at[field, FIRST + 2 * planes - 1, part, pl.ds(0, lanes)],
+                      last_send.at[2 * r + field], last_recv.at[2 * r + field], grow=gi - 1)
 
     def x_copies(group, slot, count):
         own = pl.ds(slot, count)
@@ -95,18 +108,9 @@
     def hole(phases):
         return 1.0 - jnp.clip(phases, -1.0, 1.0)
 
-    def advance(center, lower, upper, plane, step):
-        p, u = center
+    def update(p, u, w, total, flow, plane, step):
         height = (gi * planes + plane).astype(jnp.float32)
         temper = gradient_scale * ((height + 0.5) / grid_rows - 0.5) - drift_rate * step
-        w = hole(p)
-        total = lower[0] + upper[0]
-        flow = flux(w, u, hole(lower[0]), lower[1]) + flux(w, u, hole(upper[0]), upper[1])
-        for axis, size in ((0, tall), (1, wide)):
-            pn, un = pltpu.roll(p, size - 1, axis), pltpu.roll(u, size - 1, axis)
-            total = total + pn + pltpu.roll(p, 1, axis)
-            f = flux(w, u, hole(pn), un)
-            flow = flow + f - pltpu.roll(f, 1, axis)
         laplace = (total - 6.0 * p) * (1.0 / spacing_sq)
         room = 1.0 - p * p
         driving = laplace + p * room - coupling * (room * room) * (u + temper)
@@ -116,6 +120,37 @@
         weight = 2.0 * partition + (1.0 - partition) * w
         return p + change, u + gain / weight
 
+    def along(p, u, w, axis, size):
+        pn, un = pltpu.roll(p, size - 1, axis), pltpu.roll(u, size - 1, axis)
+        f = flux(w, u, hole(pn), un)
+        return pn + pltpu.roll(p, 1, axis), f - pltpu.roll(f, 1, axis)
+
+    def advance(center, lower, upper, plane, step):
+        p, u = center
+        w = hole(p)
+        total = lower[0] + upper[0]
+        flow = flux(w, u, hole(lower[0]), lower[1]) + flux(w, u, hole(upper[0]), upper[1])
+        for axis, size in ((0, tall), (1, wide)):
+            t, f = along(p, u, w, axis, size)
+            total, flow = total + t, flow + f
+        return update(p, u, w, total, flow, plane, step)
+
+    def tile(buf, slot, r):
+        part = pl.ds(TILE * r, TILE)
+        return buf[0, slot, part, :], buf[1, slot, part, :]
+
+    def advance_tile(buf, slot, r, lower, upper, plane, step):
+        count = tall // TILE
+        p, u = tile(buf, slot, r)
+        before, after = tile(buf, slot, (r - 1) % count), tile(buf, slot, (r + 1) % count)
+        w = hole(p)
+        total, flow = along(p, u, w, 1, wide)
+        pb, ub = (pltpu.roll(jnp.concatenate([a, b]), 1, 0)[TILE:] for a, b in zip(before, (p, u)))
+        pa, ua = (pltpu.roll(jnp.concatenate([b, a]), 2 * TILE - 1, 0)[:TILE] for a, b in zip(after, (p, u)))
+        for pn, un in ((pb, ub), (pa, ua), lower, upper):
+            total, flow = total + pn, flow + flux(w, u, hole(pn), un)
+        return update(p, u, w, total, flow, plane, step)
+
     def pick(cond, a, b):
         return tuple(jnp.where(cond, x, y) for x, y in zip(a, b))
 
@@ -172,24 +207,26 @@
     for edge, near in ((at_bottom, gi - 1), (at_top, gi + 1)):
         @pl.when(jnp.logical_not(edge))
         def _():
-            for where in (dict(grow=near), dict(grow=near, cross=c_next), dict(grow=near, cross=c_prev)):
-                pl.semaphore_signal(barrier, inc=1, device_id=where, device_id_type=MESH)
+            pl.semaphore_signal(barrier, inc=1, device_id=dict(grow=near), device_id_type=MESH)
 
     ends = at_bottom.astype(jnp.int32) + at_top.astype(jnp.int32)
-    pl.semaphore_wait(barrier, 10 - 3 * ends)
+    pl.semaphore_wait(barrier, 6 - ends)
 
     fields = range(2)
     has_lower, has_upper = jnp.logical_not(at_bottom), jnp.logical_not(at_top)
 
     @pl.when(has_lower)
     def _():
-        for plane in range(planes):
+        for plane in range(planes - 1):
             for f in fields:
                 z_down(f, plane).start()
             if plane == 0:
                 for f in fields:
-                    for c in y_diag(f):
+                    for c in z_edge(f):
                         c.start()
+        for r in range(rows // TILE):
+            for f in fields:
+                z_last(f, r).start()
 
     @pl.when(has_upper)
     def _():
@@ -256,6 +293,11 @@
         for f in fields:
             z_down(f, 1).wait_recv()
         start_y(2, above + 1)
+        for f in fields:
+            for c in z_edge(f):
+                c.wait_recv()
+        for side in range(2):
+            y_edge(side).start()
 
     @pl.when(has_lower)
     def _():
@@ -284,8 +326,8 @@
         pass_x(2, above + 1)
         for f in fields:
             z_down(f, 2).wait_recv()
-            for c in y_diag(f):
-                c.wait_recv()
+        for side in range(2):
+            y_edge(side).wait_recv()
         for c in x_copies(4, above + 2, 1):
             c.start()
         finish_x(2, above + 1)
@@ -305,15 +347,18 @@
     put2(4, pick(jnp.logical_and(at_top, jnp.logical_not(moved_early)), t0(4), t2(4)))
     step2(3)
 
-    @pl.when(has_upper)
-    def _():
-        for f in fields:
-            z_down(f, 3).wait_recv()
-
-    step0(6)
-    step1(5)
-    put2(5, pick(at_top, t2(4), t2(5)))
-    step2(4)
+    for r in range(rows // TILE):
+        @pl.when(has_upper)
+        def _():
+            for f in fields:
+                z_last(f, r).wait_recv()
+
+        v1 = advance_tile(start, FIRST + 6, r, tile(start, FIRST + 5, r), tile(start, FIRST + 7, r), 6, 0)
+        v2 = advance_tile(one, 6, r, tile(one, 5, r), v1, 5, 1)
+        v2 = pick(at_top, tile(two, 4, r), v2)
+        a, b = advance_tile(two, 4, r, tile(two, 3, r), v2, 4, 2)
+        phi_out[3, pl.ds(TILE * r, TILE)] = a[:, :lanes]
+        sol_out[3, pl.ds(TILE * r, TILE)] = b[:, :lanes]
 
     for c in own_y + list(own_x):
         c.wait_send()
@@ -322,12 +367,13 @@
 
     @pl.when(has_lower)
     def _():
-        for plane in range(planes):
-            for f in fields:
+        for f in fields:
+            for plane in range(planes - 1):
                 z_down(f, plane).wait_send()
-        for f in fields:
-            for c in y_diag(f):
+            for c in z_edge(f):
                 c.wait_send()
+            for r in range(rows // TILE):
+                z_last(f, r).wait_send()
         for c in y_relay(0, below) + x_copies(1, below, 1):
             c.wait_send()
 
@@ -336,6 +382,8 @@
         for k in range(2):
             for f in fields:
                 z_up(f, k).wait_send()
+        for side in range(2):
+            y_edge(side).wait_send()
         for c in y_relay(2, above + 1) + x_copies(3, above + 1, 1) + x_copies(4, above + 2, 1):
             c.wait_send()
 
@@ -367,8 +415,9 @@
             pltpu.VMEM((2, slots, tall, COL), jnp.float32),
             pltpu.VMEM((2, planes + 4, tall, wide), jnp.float32),
             pltpu.VMEM((2, planes + 2, tall, wide), jnp.float32),
+            pltpu.VMEM((2, 2, TILE, lanes), jnp.float32),
             pltpu.VMEM((rows, lanes), jnp.int32),
-            dma((3,)), dma((4,)), dma((4,)), dma((2 * (planes + 2),)), dma((2 * (planes + 2),)),
+            dma((3,)), dma((6,)), dma((6,)), dma((rows // 4,)), dma((rows // 4,)), dma((2 * (planes + 2),)), dma((2 * (planes + 2),)),
             dma((4,)), dma((4,)), dma((6,)), dma((6,)), dma((10,)), dma((10,)),
         ],
         compiler_params=pltpu.CompilerParams(collective_id=0, has_side_effects=True),

time: 21.7 us -> 21.8 us (level)
  no operation moved by 1% of the time
where the time goes in v4:
time: 21.8 us; the launch traced here: 21.4 us
  Pallas kernels  20.1 us (92%)
  between operations  1.28 us (6%)
    pallas_call x1, Pallas kernels, shards(): pl.pallas_call(functools.partial(kernel, (planes, rows, lanes)), out_shap...  19.3 us
    pallas_call x1, Pallas kernels, shards(): pl.pallas_call(write_out, out_shape=(field, field), in_specs=[vmem, vmem]...  0.81 us

profile of v4, /device:TPU:1, one launch (start us, length us, event | category | flops | bytes accessed | tf_op | source)
XLA Modules:
  0.0 21.4 jit_solution(14676221074743340021)
XLA Ops:
  1.3 19.3 %shard_map.59 = (f32[4,32,512]{2,1,0:T(8,128)S(1)}, f32[4,32,512]{2,1,0:T(8,128)S(1)}) custom-call(s32[1]{0:T(128)S(6)} %copy.6.shift_ref, s32[32,512]{1,0:T(8,128)} %seed_ref.1, f32[4,32,512]{2,1,0:T(8,128)} %phi_in.1, f32[4,32,512]{2,1,0:T(8,128)} %sol_in.1), custom_call_target="tpu_custom_call" | custom-call | tf_op jit(solution)/shard_map/pallas_call | solution.py:407
  20.6 0.8 %shard_map.60 = (f32[4,32,512]{2,1,0:T(8,128)}, f32[4,32,512]{2,1,0:T(8,128)}) custom-call(f32[4,32,512]{2,1,0:T(8,128)S(1)} %get-tuple-element.4.phi_ref, f32[4,32,512]{2,1,0:T(8,128)S(1)} %get-tuple-element.5.sol_ref), custom_call_target="tpu_custom_call" | custom-call | tf_op jit(solution)/shard_map/pallas_call | solution.py:425

commit v5 on v4

--- a/solution.py
+++ b/solution.py
@@ -42,15 +42,20 @@
         return pltpu.make_async_remote_copy(src_ref=src, dst_ref=dst, send_sem=send, recv_sem=recv,
                                             device_id=where, device_id_type=MESH)
 
-    def z_down(field, plane):
-        n = 2 * plane + field
-        return remote(inputs[field].at[plane], start.at[(field, FIRST + planes + plane) + inside],
-                      z_send.at[n], z_recv.at[n], grow=gi - 1)
-
-    def z_up(field, k):
-        n = 2 * (planes + k) + field
-        return remote(inputs[field].at[planes - 1 - k], start.at[(field, FIRST - 1 - k) + inside],
-                      z_send.at[n], z_recv.at[n], grow=gi + 1)
+    pieces = ((0, TILE), (rows - TILE, TILE), (TILE, rows - 2 * TILE))
+
+    def z_piece(field, plane, slot, which, order, near):
+        first, count = pieces[which]
+        part = pl.ds(first, count)
+        n = len(pieces) * (2 * order + field) + which
+        return remote(inputs[field].at[plane, part, :], start.at[field, slot, part, pl.ds(0, lanes)],
+                      z_send.at[n], z_recv.at[n], grow=near)
+
+    def z_down(field, plane, which):
+        return z_piece(field, plane, FIRST + planes + plane, which, plane, gi - 1)
+
+    def z_up(field, k, which):
+        return z_piece(field, planes - 1 - k, FIRST - 1 - k, which, planes + k, gi + 1)
 
     def y_pair(src_of, dst_of, count, send, recv, first, **where):
         low = remote(src_of(pl.ds(0, count)), dst_of(pl.ds(rows, count)),
@@ -218,8 +223,9 @@
     @pl.when(has_lower)
     def _():
         for plane in range(planes - 1):
-            for f in fields:
-                z_down(f, plane).start()
+            for which in range(3):
+                for f in fields:
+                    z_down(f, plane, which).start()
             if plane == 0:
                 for f in fields:
                     for c in z_edge(f):
@@ -231,8 +237,9 @@
     @pl.when(has_upper)
     def _():
         for k in range(2):
-            for f in fields:
-                z_up(f, k).start()
+            for which in range(3):
+                for f in fields:
+                    z_up(f, k, which).start()
 
     own_y = [c for f in fields for c in y_own(f)]
     for c in own_y:
@@ -247,6 +254,13 @@
 
     below, above = FIRST - 1, FIRST + planes
 
+    def arrived(copy_of, k, parts):
+        for which in parts:
+            for f in fields:
+                copy_of(f, k, which).wait_recv()
+
+    edge_parts, middle, whole = (0, 1), (2,), (0, 1, 2)
+
     def start_y(group, slot):
         for c in y_relay(group, slot):
             c.start()
@@ -266,14 +280,12 @@
 
     @pl.when(has_lower)
     def _():
-        for f in fields:
-            z_up(f, 0).wait_recv()
+        arrived(z_up, 0, edge_parts)
         start_y(0, below)
 
     @pl.when(has_upper)
     def _():
-        for f in fields:
-            z_down(f, 0).wait_recv()
+        arrived(z_down, 0, edge_parts)
 
     start_y(1, above)
     for c in own_x:
@@ -284,14 +296,18 @@
 
     @pl.when(has_lower)
     def _():
+        arrived(z_up, 0, middle)
         pass_x(0, below)
 
+    @pl.when(has_upper)
+    def _():
+        arrived(z_down, 0, middle)
+
     pass_x(1, above)
 
     @pl.when(has_upper)
     def _():
-        for f in fields:
-            z_down(f, 1).wait_recv()
+        arrived(z_down, 1, edge_parts)
         start_y(2, above + 1)
         for f in fields:
             for c in z_edge(f):
@@ -312,8 +328,7 @@
 
     @pl.when(has_lower)
     def _():
-        for f in fields:
-            z_up(f, 1).wait_recv()
+        arrived(z_up, 1, whole)
 
     step0(-1)
     put1(-1, pick(at_bottom, t1(0), t1(-1)))
@@ -323,9 +338,9 @@
 
     @pl.when(has_upper)
     def _():
+        arrived(z_down, 1, middle)
         pass_x(2, above + 1)
-        for f in fields:
-            z_down(f, 2).wait_recv()
+        arrived(z_down, 2, whole)
         for side in range(2):
             y_edge(side).wait_recv()
         for c in x_copies(4, above + 2, 1):
@@ -369,7 +384,8 @@
     def _():
         for f in fields:
             for plane in range(planes - 1):
-                z_down(f, plane).wait_send()
+                for which in range(3):
+                    z_down(f, plane, which).wait_send()
             for c in z_edge(f):
                 c.wait_send()
             for r in range(rows // TILE):
@@ -381,7 +397,8 @@
     def _():
         for k in range(2):
             for f in fields:
-                z_up(f, k).wait_send()
+                for which in range(3):
+                    z_up(f, k, which).wait_send()
         for side in range(2):
             y_edge(side).wait_send()
         for c in y_relay(2, above + 1) + x_copies(3, above + 1, 1) + x_copies(4, above + 2, 1):
@@ -417,7 +434,7 @@
             pltpu.VMEM((2, planes + 2, tall, wide), jnp.float32),
             pltpu.VMEM((2, 2, TILE, lanes), jnp.float32),
             pltpu.VMEM((rows, lanes), jnp.int32),
-            dma((3,)), dma((6,)), dma((6,)), dma((rows // 4,)), dma((rows // 4,)), dma((2 * (planes + 2),)), dma((2 * (planes + 2),)),
+            dma((3,)), dma((6,)), dma((6,)), dma((rows // 4,)), dma((rows // 4,)), dma((6 * (planes + 2),)), dma((6 * (planes + 2),)),
             dma((4,)), dma((4,)), dma((6,)), dma((6,)), dma((10,)), dma((10,)),
         ],
         compiler_params=pltpu.CompilerParams(collective_id=0, has_side_effects=True),

time: 21.8 us -> 21.1 us (0.968)
  Pallas kernels: 20.1 us -> 19.5 us
    pallas_call x1, Pallas kernels: 19.3 us -> 18.7 us  [shards(): pl.pallas_call(functools.partial(kernel, (planes, rows, lanes)), out_shap...]
where the time goes in v5:
time: 21.1 us; the launch traced here: 20.8 us
  Pallas kernels  19.5 us (92%)
  between operations  1.28 us (6%)
    pallas_call x1, Pallas kernels, shards(): pl.pallas_call(functools.partial(kernel, (planes, rows, lanes)), out_shap...  18.7 us
    pallas_call x1, Pallas kernels, shards(): pl.pallas_call(write_out, out_shape=(field, field), in_specs=[vmem, vmem]...  0.81 us

profile of v5, /device:TPU:1, one launch (start us, length us, event | category | flops | bytes accessed | tf_op | source)
XLA Modules:
  0.0 20.8 jit_solution(18170811092757503783)
XLA Ops:
  1.3 18.7 %shard_map.59 = (f32[4,32,512]{2,1,0:T(8,128)S(1)}, f32[4,32,512]{2,1,0:T(8,128)S(1)}) custom-call(s32[1]{0:T(128)S(6)} %copy.6.shift_ref, s32[32,512]{1,0:T(8,128)} %seed_ref.1, f32[4,32,512]{2,1,0:T(8,128)} %phi_in.1, f32[4,32,512]{2,1,0:T(8,128)} %sol_in.1), custom_call_target="tpu_custom_call" | custom-call | tf_op jit(solution)/shard_map/pallas_call | solution.py:424
  20.0 0.8 %shard_map.60 = (f32[4,32,512]{2,1,0:T(8,128)}, f32[4,32,512]{2,1,0:T(8,128)}) custom-call(f32[4,32,512]{2,1,0:T(8,128)S(1)} %get-tuple-element.4.phi_ref, f32[4,32,512]{2,1,0:T(8,128)S(1)} %get-tuple-element.5.sol_ref), custom_call_target="tpu_custom_call" | custom-call | tf_op jit(solution)/shard_map/pallas_call | solution.py:442

commit v6 on v5

--- a/solution.py
+++ b/solution.py
@@ -220,19 +220,21 @@
     fields = range(2)
     has_lower, has_upper = jnp.logical_not(at_bottom), jnp.logical_not(at_top)
 
-    @pl.when(has_lower)
-    def _():
-        for plane in range(planes - 1):
-            for which in range(3):
-                for f in fields:
-                    z_down(f, plane, which).start()
-            if plane == 0:
-                for f in fields:
-                    for c in z_edge(f):
-                        c.start()
-        for r in range(rows // TILE):
+    def start_down(plane):
+        for which in range(3):
             for f in fields:
-                z_last(f, r).start()
+                z_down(f, plane, which).start()
+
+    @pl.when(has_lower)
+    def _():
+        start_down(0)
+        for f in fields:
+            for c in z_edge(f):
+                c.start()
+
+    own_y = [c for f in fields for c in y_own(f)]
+    for c in own_y:
+        c.start()
 
     @pl.when(has_upper)
     def _():
@@ -241,9 +243,14 @@
                 for f in fields:
                     z_up(f, k, which).start()
 
-    own_y = [c for f in fields for c in y_own(f)]
-    for c in own_y:
-        c.start()
+    @pl.when(has_lower)
+    def _():
+        for plane in range(1, planes - 1):
+            start_down(plane)
+        for r in range(rows // TILE):
+            for f in fields:
+                z_last(f, r).start()
+
     for copy in own_copies:
         copy.wait()
     for c in own_y:

time: 21.1 us -> 21.1 us (level)
  no operation moved by 1% of the time
where the time goes in v6:
time: 21.1 us; the launch traced here: 20.8 us
  Pallas kernels  19.5 us (92%)
  between operations  1.28 us (6%)
    pallas_call x1, Pallas kernels, shards(): pl.pallas_call(functools.partial(kernel, (planes, rows, lanes)), out_shap...  18.7 us
    pallas_call x1, Pallas kernels, shards(): pl.pallas_call(write_out, out_shape=(field, field), in_specs=[vmem, vmem]...  0.81 us

profile of v6, /device:TPU:1, one launch (start us, length us, event | category | flops | bytes accessed | tf_op | source)
XLA Modules:
  0.0 20.8 jit_solution(8206056591952881321)
XLA Ops:
  1.3 18.7 %shard_map.59 = (f32[4,32,512]{2,1,0:T(8,128)S(1)}, f32[4,32,512]{2,1,0:T(8,128)S(1)}) custom-call(s32[1]{0:T(128)S(6)} %copy.6.shift_ref, s32[32,512]{1,0:T(8,128)} %seed_ref.1, f32[4,32,512]{2,1,0:T(8,128)} %phi_in.1, f32[4,32,512]{2,1,0:T(8,128)} %sol_in.1), custom_call_target="tpu_custom_call" | custom-call | tf_op jit(solution)/shard_map/pallas_call | solution.py:431
  20.0 0.8 %shard_map.60 = (f32[4,32,512]{2,1,0:T(8,128)}, f32[4,32,512]{2,1,0:T(8,128)}) custom-call(f32[4,32,512]{2,1,0:T(8,128)S(1)} %get-tuple-element.4.phi_ref, f32[4,32,512]{2,1,0:T(8,128)S(1)} %get-tuple-element.5.sol_ref), custom_call_target="tpu_custom_call" | custom-call | tf_op jit(solution)/shard_map/pallas_call | solution.py:449
